TPU v7x, 32 devices: a whole 2x2x4 slice. The times are simulated.
32 devices in a mesh: step: 2 (over core), tile: 16 (over z, y, x).
Axes of the slice: x: 2, y: 2, z: 4, core: 2. Of those that a mesh axis runs over, the one named last changes fastest.
Arguments:
- latents: float32 [2, 2048, 3072], P('step', 'tile'), may hold values from -6 to 6
- start: float32 [2048, 3072], P('tile'), may hold values from -6 to 6
- cached_velocity: float32 [2, 2048, 3072], P('step', 'tile'), may hold values from -4 to 4
- shift: float32 [2, 3072], P('step'), may hold values from -3 to 3
- scale: float32 [2, 3072], P('step'), may hold values from -3 to 3
- gate: float32 [2, 3072], P('step'), may hold values from -10 to 10
- step_sizes: float32 [2], P('step'), may hold values from 0.1 to 0.5
- converged: int32 [2, 16], P(None, 'tile'), may hold values from 0 to 1, as said below
- neighbours: int32 [16, 4], P('tile'), may hold values from 0 to 1, as said below
- w_qkv: bfloat16 [3, 3072, 2048], P(None, None, 'step'), may hold values from -0.109375 to 0.109375
- q_gain: float32 [128], replicated, may hold values from 0.1 to 1.9
- k_gain: float32 [128], replicated, may hold values from 0.1 to 1.9
- w_out: bfloat16 [2048, 3072], P('step', 'tile'), may hold values from -0.5 to 0.5
Outputs:
- updated: float32 [2, 2048, 3072], P('step', 'tile')
- velocity: float32 [2, 2048, 3072], P('step', 'tile')
Inputs may be any that keep to these rules, and one draw needn't show every extreme that they name: For each tile the converged steps are the first ones of the window, at most 1 of them. `neighbours`: an entry is 0 wherever the grid of 4 rows of 4 tiles has no neighbour that way.
All inputs are finite; a program needn't handle non-finite values.
Results may differ from a plain program's by a relative error of at most 0.008.
Values may be sent and summed in bfloat16 or wider, within the bound.
A program may use at most 128 MiB of HBM per device.

v0:
```python
import jax
import jax.numpy as jnp
from jax import lax
from jax.sharding import PartitionSpec as P

GRID_COLS = 4


def shifted(value, axis, steps):
    count = lax.axis_size(axis)
    first, last = (max(0, -steps), min(count, count - steps))
    return lax.ppermute(value, axis, [(source, source + steps) for source in range(first, last)])


def entering(value, axis, join, neutral):
    place = lax.axis_index(axis)
    gathered = lax.all_gather(value.astype(jnp.bfloat16), axis)
    state = jnp.zeros_like(value) + jnp.asarray(neutral, value.dtype)

    def one(lap, state):
        return join(state, lax.dynamic_index_in_dim(gathered, lap, 0, False).astype(value.dtype))

    return lax.fori_loop(0, place, one, state)


def attend(queries, keys_all, values_all, key_mask, factor):
    scores = (
        jnp.einsum("sqhd,skhd->shqk", queries, keys_all, preferred_element_type=jnp.float32)
        * factor
    )
    expo = jnp.exp(scores) * key_mask
    probs = (expo / jnp.sum(expo, axis=-1, keepdims=True)).astype(jnp.bfloat16)
    attended = jnp.einsum("shqk,skhd->sqhd", probs, values_all, preferred_element_type=jnp.float32)
    return attended.astype(jnp.bfloat16)


def rms_gain(block, gain):
    return (
        block / jnp.sqrt(jnp.mean(block * block, axis=-1, keepdims=True) + 1e-06) * gain
    ).astype(jnp.bfloat16)


def add_terms(earlier, later):
    return earlier + later


def body(
    latents,
    start,
    cached_velocity,
    shift,
    scale,
    gate,
    step_sizes,
    converged,
    neighbours,
    w_qkv,
    q_gain,
    k_gain,
    w_out,
):
    tile_tokens = latents.shape[1]
    width = latents.shape[2]
    group_cols = w_qkv.shape[2]
    head_size = q_gain.shape[0]
    group_heads = group_cols // head_size
    step_count = converged.shape[0]
    own = latents[0]
    mean = jnp.mean(own, axis=-1, keepdims=True)
    var = jnp.mean(jnp.square(own - mean), axis=-1, keepdims=True)
    normed = ((own - mean) / jnp.sqrt(var + 1e-06) * (1.0 + scale) + shift).astype(jnp.bfloat16)[
        None
    ]
    block = lax.all_gather(normed, "step", axis=0, tiled=True)
    count = block.shape[0]
    project_flat = block.reshape(count * tile_tokens, width)
    result = jnp.einsum("rd,cdf->crf", project_flat, w_qkv, preferred_element_type=jnp.float32)
    qkv = result.reshape(3, count, tile_tokens, group_cols)
    qkv = qkv.reshape(3, step_count, tile_tokens, group_heads, head_size)
    queries = rms_gain(qkv[0], q_gain)
    keys_own = rms_gain(qkv[1], k_gain)
    values_own = qkv[2].astype(jnp.bfloat16)
    stacked = jnp.stack([keys_own, values_own]).reshape(2, step_count, tile_tokens, group_cols)
    collected = [stacked]
    for offset in (1, -1, GRID_COLS, -GRID_COLS):
        collected.append(shifted(stacked, "tile", offset))
    joined = jnp.concatenate(collected, axis=2).reshape(
        2, step_count, 5 * tile_tokens, group_heads, head_size
    )
    key_mask = jnp.concatenate(
        [
            jnp.ones((tile_tokens,), jnp.float32),
            jnp.repeat(neighbours[0].astype(jnp.float32), tile_tokens),
        ]
    )
    factor = 1.0 / jnp.sqrt(jnp.float32(head_size))
    results = []
    for position in range(step_count):

        def fresh(_, position=position):
            return attend(
                queries[position : position + 1],
                joined[0, position : position + 1],
                joined[1, position : position + 1],
                key_mask,
                factor,
            )

        def blank(_, position=position):
            return jnp.zeros((1, tile_tokens, group_heads, head_size), jnp.bfloat16)

        results.append(lax.cond(converged[position, 0] > 0, blank, fresh, 0))
    attended = jnp.concatenate(results, axis=0)
    attended = attended.reshape(step_count, tile_tokens, group_cols)
    flat = attended.reshape(step_count * tile_tokens, group_cols)
    terms = jnp.dot(
        flat, lax.all_gather(w_out, "tile", axis=1, tiled=True), preferred_element_type=jnp.float32
    )
    terms = terms.reshape(step_count, tile_tokens, width)
    projected = lax.psum_scatter(
        terms.astype(jnp.bfloat16), "step", scatter_dimension=0, tiled=True
    ).astype(jnp.float32)
    here = lax.axis_index("step")
    flag = lax.dynamic_slice_in_dim(converged, here, 1, 0)[0, 0]
    velocity = jnp.where(flag > 0, cached_velocity, gate[:, None, :] * projected)
    scaled = step_sizes[:, None, None] * velocity
    prefix = entering(scaled, "step", add_terms, jnp.zeros_like(scaled))
    updated = start[None, :, :] + prefix
    return (updated, velocity)


def solution(mesh):
    placed = (
        P("step", "tile", None),
        P("tile", None),
        P("step", "tile", None),
        P("step", None),
        P("step", None),
        P("step", None),
        P("step"),
        P(None, "tile"),
        P("tile", None),
        P(None, None, "step"),
        P(),
        P(),
        P("step", "tile"),
    )
    return jax.shard_map(
        body,
        mesh=mesh,
        in_specs=placed,
        out_specs=(P("step", "tile", None), P("step", "tile", None)),
        check_vma=False,
    )
```

profile of v0, /device:TPU:3, one launch (start us, length us, event | category | flops | bytes accessed | tf_op | source)
XLA Modules:
  0.0 182.7 jit_solution(4044287068420179241)
XLA Ops:
  7.2 0.0 copy-start
  7.2 0.0 all-gather.5.cloned.1.call-start
  7.3 1.7 reduce_sum.54
  8.9 0.1 copy-done.2
  9.1 0.3 fusion.22
  9.4 0.0 copy-done.5
  9.4 1.2 add_convert_fusion
  10.6 0.0 all-gather.5.cloned.1.call-update
  10.7 0.0 all-gather.7.cloned.1.call-start
  10.7 0.7 all-gather.7.cloned.1.call-update
  11.4 0.0 reduce-scatter.2.cloned.1.call-start
  11.5 11.1 %all-gather.5.cloned.1.call-done = bf16[2,128,3072]{2,1,0:T(8,128)(2,1)} async-done(((bf16[1,128,3072]{2,1,0:T(8,128)(2,1)}), bf16[2,128,3072]{2,1,0:T(8,128)(2,1)}) %all-gather.5.cloned.1.call-update) | async-done | bytes 1572880 | tf_op jit(solution)/shard_map/all_gather | solution.py:74
  22.6 9.4 %convolution_bitcast_fusion = f32[3,256,1024]{2,1,0:T(8,128)S(1)} fusion(bf16[256,3072,1]{1,0,2:T(8,128)(2,1)} %bitcast.125, bf16[3,3072,1024]{2,1,0:T(8,128)(2,1)} %param.28), kind=kOutput, calls=%fused_computation.28 | convolution fusion | flops 4831838208 | bytes 23592960 | tf_op jit(solution)/shard_map/rd,cdf->crf/dot_general | solution.py:77
  32.0 0.9 slice.76
  32.9 0.3 multiply_bitcast_fusion
  33.2 0.2 copy.46
  33.4 0.3 bitcast_reduce_fusion
  33.7 0.1 copy.37
  33.8 0.3 copy.38
  34.1 1.4 copy.39
  35.5 0.0 copy-start.10
  35.5 0.0 copy-start.8
  35.5 0.2 fusion.24
  35.7 0.0 copy-start.9
  35.8 1.3 pad_maximum_fusion
  37.1 3.1 %collective-permute-start = (bf16[2,2,128,1024]{2,3,1,0:T(8,128)(2,1)S(1)}, bf16[2,2,128,1024]{2,3,1,0:T(8,128)(2,1)}, u32[]{:S(2)}, u32[]{:S(2)}) collective-permute-start(bf16[2,2,128,1024]{2,3,1,0:T(8,128)(2,1)S(1)} %get-tuple-element.101), channel_id=1, source_target_pairs={{0,1},{1,2},{2,3},{3,4},{4,5},{5,6},{6,7},{7,8},{8,9},{9,10},{10,1... | collective-permute-start | bytes 3145736 | tf_op jit(solution)/shard_map/ppermute | solution.py:12
  40.2 0.0 copy-done.10
  40.2 3.2 %collective-permute-start.1 = (bf16[2,2,128,1024]{2,3,1,0:T(8,128)(2,1)S(1)}, bf16[2,2,128,1024]{2,3,1,0:T(8,128)(2,1)}, u32[]{:S(2)}, u32[]{:S(2)}) collective-permute-start(bf16[2,2,128,1024]{2,3,1,0:T(8,128)(2,1)S(1)} %get-tuple-element.101), channel_id=1, source_target_pairs={{1,0},{2,1},{3,2},{4,3},{5,4},{6,5},{7,6},{8,7},{9,8},{10,9},{11,1... | collective-permute-start | bytes 3145736 | tf_op jit(solution)/shard_map/ppermute | solution.py:12
  43.4 0.6 constant_dynamic-slice_fusion
  45.3 3.1 %collective-permute-start.2 = (bf16[2,2,128,1024]{2,3,1,0:T(8,128)(2,1)S(1)}, bf16[2,2,128,1024]{2,3,1,0:T(8,128)(2,1)}, u32[]{:S(2)}, u32[]{:S(2)}) collective-permute-start(bf16[2,2,128,1024]{2,3,1,0:T(8,128)(2,1)S(1)} %get-tuple-element.101), channel_id=1, source_target_pairs={{0,4},{1,5},{2,6},{3,7},{4,8},{5,9},{6,10},{7,11},{8,12},{9,13},{1... | collective-permute-start | bytes 3145736 | tf_op jit(solution)/shard_map/ppermute | solution.py:12
  48.4 0.1 broadcast_bitcast_fusion.1
  48.5 1.3 collective-permute-start.3
  49.8 0.2 copy.45
  50.0 0.3 multiply_reduce_fusion
  50.3 0.1 copy.35
  50.4 0.0 copy-done.9
  50.4 0.3 fusion.26
  50.8 46.5 %collective-permute-done = bf16[2,2,128,1024]{2,3,1,0:T(8,128)(2,1)} collective-permute-done((bf16[2,2,128,1024]{2,3,1,0:T(8,128)(2,1)S(1)}, bf16[2,2,128,1024]{2,3,1,0:T(8,128)(2,1)}, u32[]{:S(2)}, u32[]{:S(2)}) %collective-permute-start) | collective-permute-done | bytes 1048608 | tf_op jit(solution)/shard_map/ppermute | solution.py:12
  97.3 2.3 %constant_dynamic-update-slice_fusion.3 = bf16[2,2,640,1024]{2,3,1,0:T(8,128)(2,1)} fusion(bf16[2,2,640,1024]{2,3,1,0:T(8,128)(2,1)} %get-tuple-element.102, bf16[2,2,128,1024]{2,3,1,0:T(8,128)(2,1)} %collective-permute-done), kind=kLoop, calls=%fused_computation.54 | loop fusion | bytes 2097152
  99.5 0.0 collective-permute-done.1
  99.5 2.3 %constant_dynamic-update-slice_fusion.2 = bf16[2,2,640,1024]{2,3,1,0:T(8,128)(2,1)} fusion(bf16[2,2,640,1024]{2,3,1,0:T(8,128)(2,1)} %constant_dynamic-update-slice_fusion.3, bf16[2,2,128,1024]{2,3,1,0:T(8,128)(2,1)} %collective-permute-done.1), kind=kLoop, calls=%fused_computation.53 | loop fusion | bytes 2097152
  101.9 0.0 collective-permute-done.2
  101.9 2.4 %constant_dynamic-update-slice_fusion.1 = bf16[2,2,640,1024]{2,3,1,0:T(8,128)(2,1)} fusion(bf16[2,2,640,1024]{2,3,1,0:T(8,128)(2,1)} %constant_dynamic-update-slice_fusion.2, bf16[2,2,128,1024]{2,3,1,0:T(8,128)(2,1)} %collective-permute-done.2), kind=kLoop, calls=%fused_computation.52 | loop fusion | bytes 2097152
  104.3 0.0 collective-permute-done.3
  104.3 2.4 %constant_dynamic-update-slice_fusion = bf16[2,2,640,1024]{2,3,1,0:T(8,128)(2,1)} fusion(bf16[2,2,640,1024]{2,3,1,0:T(8,128)(2,1)} %constant_dynamic-update-slice_fusion.1, bf16[2,2,128,1024]{2,3,1,0:T(8,128)(2,1)} %collective-permute-done.3), kind=kLoop, calls=%fused_computation.51 | loop fusion | bytes 2097152 | tf_op jit(solution)/shard_map/concatenate | solution.py:87
  106.7 12.1 %conditional.3 = (bf16[1,128,8,128]{3,1,2,0:T(8,128)(2,1)S(1)}) conditional(s32[]{:T(128)} %bitcast.31, (bf16[2,128,8,128]{3,1,2,0:T(8,128)(2,1)S(1)}, bf16[2,2,640,8,128]{2,4,3,1,0:T(8,128)(2,1)}, f32[640]{0:T(1024)S(1)}) %tuple.71, () %tuple.26), branch_computations={%region_7.0_spmd, %region_9.0_spmd} | conditional | flops 340261888 | bytes 18889224 | solution.py:112
  106.7 7.9 %copy.41 = bf16[2,2,640,8,128]{4,2,3,1,0:T(8,128)(2,1)} copy(bf16[2,2,640,8,128]{2,4,3,1,0:T(8,128)(2,1)} %get-tuple-element.78) | data formatting | bytes 10485760 | tf_op jit(solution)/shard_map
  114.6 2.1 %fusion.8 = (f32[8,128]{1,0:T(8,128)S(1)}, f32[8,128,640]{2,1,0:T(8,128)S(1)}) fusion(f32[640]{0:T(1024)S(1)} %get-tuple-element.39, bf16[2,2,640,8,128]{4,2,3,1,0:T(8,128)(2,1)} %copy.41, bf16[2,128,8,128]{3,1,2,0:T(8,128)(2,1)S(1)} %get-tuple-element.37), kind=kOutput, calls=%fused_computation.14 | convolution fusion | flops 169737216 | bytes 4202496 | tf_op jit(solution)/shard_map/cond/branch_0_fun/sqhd,skhd->shqk/dot_general | solution.py:28
  116.7 2.1 %fusion.12 = bf16[1,128,8,128]{3,1,2,0:T(8,128)(2,1)S(1)} fusion(bf16[2,2,640,8,128]{4,2,3,1,0:T(8,128)(2,1)} %copy.41, f32[8,128,640]{2,1,0:T(8,128)S(1)} %get-tuple-element.97, f32[8,128]{1,0:T(8,128)S(1)} %get-tuple-element.96, f32[640]{0:T(1024)S(1)} %get-tuple-element.39), kind=kOutput, calls=%fused_computation.20 | convolution fusion | flops 170524672 | bytes 4200960 | tf_op jit(solution)/shard_map/cond/branch_0_fun/shqk,skhd->sqhd/dot_general | solution.py:33
  118.8 0.0 copy-start.7
  118.8 24.6 %all-gather.7.cloned.1.call-done = bf16[1024,3072]{0,1:T(8,128)(2,1)} async-done(((bf16[1024,192]{0,1:T(8,128)(2,1)}), bf16[1024,3072]{0,1:T(8,128)(2,1)}) %all-gather.7.cloned.1.call-update) | async-done | bytes 6291472 | tf_op jit(solution)/shard_map/all_gather | solution.py:117
  143.4 5.8 %fusion.18 = bf16[2,128,3072]{2,1,0:T(8,128)(2,1)} fusion(bf16[1024,3072]{0,1:T(8,128)(2,1)} %all-gather.7.cloned.1.call-done, bf16[1,128,8,128]{3,1,2,0:T(8,128)(2,1)S(1)} %get-tuple-element.154, bf16[1,128,8,128]{3,1,2,0:T(8,128)(2,1)S(1)} %get-tuple-element.153), kind=kOutput, calls=%fused_computation.27 | convolution fusion | flops 1611661312 | bytes 8388608 | tf_op jit(solution)/shard_map/dot_general | solution.py:116
  149.2 0.0 reduce-scatter.2.cloned.1.call-update
  149.2 0.0 all-gather.9.cloned.1.call-start
  150.7 8.2 %reduce-scatter.2.cloned.1.call-done = bf16[1,128,3072]{2,1,0:T(8,128)(2,1)} async-done(((bf16[2,128,3072]{2,1,0:T(8,128)(2,1)}), bf16[1,128,3072]{2,1,0:T(8,128)(2,1)}) %reduce-scatter.2.cloned.1.call-update) | async-done | bytes 786448 | tf_op jit(solution)/shard_map/reduce_scatter | solution.py:120
  158.9 2.8 %multiply_convert_fusion = (bf16[1,128,3072]{2,1,0:T(8,128)(2,1)}, f32[1,128,3072]{2,1,0:T(8,128)}) fusion(f32[]{:T(128)} %bitcast.117, f32[1,128,3072]{2,1,0:T(8,128)S(1)} %copy-done.3, bf16[1,128,3072]{2,1,0:T(8,128)(2,1)} %reduce-scatter.2.cloned.1.call-done, f32[3072]{0:T(1024)S(1)} %bitcast.129, pred[]{:T(512)} %bitcast.15), kind=kLoop, calls=%fused_computation.33 | loop fusion | flops 1966080 | bytes 4730885 | tf_op jit(solution)/shard_map/convert_element_type | solution.py:17
  161.7 0.0 all-gather.9.cloned.1.call-update
  161.8 11.3 %all-gather.9.cloned.1.call-done = bf16[2,128,3072]{2,1,0:T(8,128)(2,1)} async-done(((bf16[1,128,3072]{2,1,0:T(8,128)(2,1)}), bf16[2,128,3072]{2,1,0:T(8,128)(2,1)}) %all-gather.9.cloned.1.call-update) | async-done | bytes 1572880 | tf_op jit(solution)/shard_map/all_gather | solution.py:17
  173.0 0.1 broadcast_in_dim.7
  173.2 0.0 copy-start.4
  173.2 1.6 while.10
  173.2 1.6 convert_add_fusion.2
  174.8 0.0 copy-start.1
  174.8 1.3 bitcast_add_fusion
  (21 shorter events, 0.2 us)
Async XLA Ops:
  7.2 4.3 %copy-start = (f32[128]{0:T(128)S(1)}, f32[128]{0:T(128)}, u32[]{:S(2)}) copy-start(f32[128]{0:T(128)} %param.30) | copy-start | bytes 1540
  7.2 1.9 %copy-start.2 = (f32[1,128,3072]{2,1,0:T(8,128)S(1)}, f32[1,128,3072]{2,1,0:T(8,128)}, u32[]{:S(2)}) copy-start(f32[1,128,3072]{2,1,0:T(8,128)} %param.19) | copy-start | bytes 4718596
  7.2 2.2 %copy-start.6 = (f32[1,3072]{1,0:T(1,128)S(1)}, f32[1,3072]{1,0:T(1,128)}, u32[]{:S(2)}) copy-start(f32[1,3072]{1,0:T(1,128)} %param.23) | copy-start | bytes 36868
  7.2 2.2 %copy-start.5 = (f32[1,3072]{1,0:T(1,128)S(1)}, f32[1,3072]{1,0:T(1,128)}, u32[]{:S(2)}) copy-start(f32[1,3072]{1,0:T(1,128)} %param.22) | copy-start | bytes 36868
  7.2 15.4 %all-gather.5.cloned.1.call-start = ((), (), s32[]{:S(2)}) async-start(), calls=%async_computation.1 | async-start | bytes 2359296 | tf_op jit(solution)/shard_map/all_gather | solution.py:74
  10.7 132.7 %all-gather.7.cloned.1.call-start = ((), (), s32[]{:S(2)}) async-start(), calls=%async_computation.2 | async-start | bytes 6684672 | tf_op jit(solution)/shard_map/all_gather | solution.py:117
  11.4 147.5 %reduce-scatter.2.cloned.1.call-start = ((), (), s32[]{:S(2)}) async-start(), calls=%async_computation.3 | async-start | bytes 2359296 | tf_op jit(solution)/shard_map/reduce_scatter | solution.py:120
  35.5 4.7 %copy-start.10 = (s32[1,4]{1,0:T(1,128)S(1)}, s32[1,4]{1,0:T(1,128)}, u32[]{:S(2)}) copy-start(s32[1,4]{1,0:T(1,128)} %param.27) | copy-start | bytes 52
  35.5 7.9 %copy-start.8 = (s32[2,1]{0,1:T(1,128)S(1)}, s32[2,1]{0,1:T(1,128)}, u32[]{:S(2)}) copy-start(s32[2,1]{0,1:T(1,128)} %param.26) | copy-start | bytes 28
  35.7 14.7 %copy-start.9 = (f32[128]{0:T(128)S(1)}, f32[128]{0:T(128)}, u32[]{:S(2)}) copy-start(f32[128]{0:T(128)} %param.29) | copy-start | bytes 1540
  37.1 60.2 %collective-permute-start = (bf16[2,2,128,1024]{2,3,1,0:T(8,128)(2,1)S(1)}, bf16[2,2,128,1024]{2,3,1,0:T(8,128)(2,1)}, u32[]{:S(2)}, u32[]{:S(2)}) collective-permute-start(bf16[2,2,128,1024]{2,3,1,0:T(8,128)(2,1)S(1)} %get-tuple-element.101), channel_id=1, source_target_pairs={{0,1},{1,2},{2,3},{3,4},{4,5},{5,6},{6,7},{7,8},{8,9},{9,10},{10,1... | collective-permute-start | bytes 3145736 | tf_op jit(solution)/shard_map/ppermute | solution.py:12
  40.2 59.4 %collective-permute-start.1 = (bf16[2,2,128,1024]{2,3,1,0:T(8,128)(2,1)S(1)}, bf16[2,2,128,1024]{2,3,1,0:T(8,128)(2,1)}, u32[]{:S(2)}, u32[]{:S(2)}) collective-permute-start(bf16[2,2,128,1024]{2,3,1,0:T(8,128)(2,1)S(1)} %get-tuple-element.101), channel_id=1, source_target_pairs={{1,0},{2,1},{3,2},{4,3},{5,4},{6,5},{7,6},{8,7},{9,8},{10,9},{11,1... | collective-permute-start | bytes 3145736 | tf_op jit(solution)/shard_map/ppermute | solution.py:12
  45.3 56.6 %collective-permute-start.2 = (bf16[2,2,128,1024]{2,3,1,0:T(8,128)(2,1)S(1)}, bf16[2,2,128,1024]{2,3,1,0:T(8,128)(2,1)}, u32[]{:S(2)}, u32[]{:S(2)}) collective-permute-start(bf16[2,2,128,1024]{2,3,1,0:T(8,128)(2,1)S(1)} %get-tuple-element.101), channel_id=1, source_target_pairs={{0,4},{1,5},{2,6},{3,7},{4,8},{5,9},{6,10},{7,11},{8,12},{9,13},{1... | collective-permute-start | bytes 3145736 | tf_op jit(solution)/shard_map/ppermute | solution.py:12
  48.5 55.8 %collective-permute-start.3 = (bf16[2,2,128,1024]{2,3,1,0:T(8,128)(2,1)S(1)}, bf16[2,2,128,1024]{2,3,1,0:T(8,128)(2,1)}, u32[]{:S(2)}, u32[]{:S(2)}) collective-permute-start(bf16[2,2,128,1024]{2,3,1,0:T(8,128)(2,1)S(1)} %get-tuple-element.101), channel_id=1, source_target_pairs={{4,0},{5,1},{6,2},{7,3},{8,4},{9,5},{10,6},{11,7},{12,8},{13,9},{1... | collective-permute-start | bytes 3145736 | tf_op jit(solution)/shard_map/ppermute | solution.py:12
  118.8 40.1 %copy-start.7 = (f32[1,3072]{1,0:T(1,128)S(1)}, f32[1,3072]{1,0:T(1,128)}, u32[]{:S(2)}) copy-start(f32[1,3072]{1,0:T(1,128)} %param.24) | copy-start | bytes 36868
  149.2 9.7 %copy-start.3 = (f32[1,128,3072]{2,1,0:T(8,128)S(1)}, f32[1,128,3072]{2,1,0:T(8,128)}, u32[]{:S(2)}) copy-start(f32[1,128,3072]{2,1,0:T(8,128)} %param.21) | copy-start | bytes 4718596
  149.2 23.8 %all-gather.9.cloned.1.call-start = ((), (), s32[]{:S(2)}) async-start(), calls=%async_computation.4 | async-start | bytes 2359296 | tf_op jit(solution)/shard_map/all_gather | solution.py:17
  173.2 1.7 copy-start.4
  174.8 1.3 copy-start.1
Sparse Core Ops, SparseCore 0:
  10.8 11.7 all-gather.4
  25.3 117.9 all-gather.6
  149.4 9.4 reduce-scatter.1
  161.9 11.0 all-gather.8
where the time goes:
time: 184 us; the launch traced here: 183 us
  waiting for transfers between devices  102 us (55%)
  local copies, waits for them, and re-layouts  21.4 us (12%)
  matrix products  19.4 us (11%)
  between operations  16.8 us (9%)
  other arithmetic  11.8 us (6%)
  starting transfers between devices  10.8 us (6%)
    ppermute x4, waiting for transfers between devices, shifted(): lax.ppermute(value, axis, [(source, source + steps) for source in range(f...  46.5 us
    all_gather x1, waiting for transfers between devices, body(): lax.all_gather(w_out, 'tile', axis=1, tiled=True)  24.6 us
    all_gather x1, waiting for transfers between devices, entering(): gathered = lax.all_gather(value.astype(jnp.bfloat16), axis)  11.3 us
    all_gather x1, waiting for transfers between devices, body(): block = lax.all_gather(normed, 'step', axis=0, tiled=True)  11.1 us
    ppermute x4, starting transfers between devices, shifted(): lax.ppermute(value, axis, [(source, source + steps) for source in range(f...  10.7 us
    dot_general x1, matrix products, body(): jnp.einsum('rd,cdf->crf', project_flat, w_qkv, preferred_element_type=jnp...  9.43 us
    reduce_scatter x1, waiting for transfers between devices, body(): lax.psum_scatter(terms.astype(jnp.bfloat16), 'step', scatter_dimension=0,...  8.22 us
    another operation x2, local copies, waits for them, and re-layouts  7.93 us
  transfers between devices with their start and end apart: 8, of which 5 were waited for; matrix products, arithmetic and copies ran while one was open for 21% of the time, Pallas kernels for 0%

commit v1 on v0

v1 whole, which is shorter than its diff:
```python
import functools
import jax
import jax.numpy as jnp
from jax import lax
from jax.experimental import pallas as pl
from jax.experimental.pallas import tpu as pltpu
from jax.sharding import PartitionSpec as P

GRID_COLS = 4
MESH = pl.DeviceIdType.MESH
BF16 = jnp.bfloat16
F32 = jnp.float32


def nearest(place, length):
    if length == 1:
        return [place]
    if length == 2:
        return [place, 1 - place]
    assert length == 4
    inner = (place * (3 - place)) // 2
    flip, turn = 3 - place, lax.rem(place + 2, 4)
    beside = place + 1 - 2 * lax.rem(place, 2)
    return [
        place,
        beside,
        inner * flip + (1 - inner) * turn,
        inner * turn + (1 - inner) * flip,
    ]


def kernel(
    tiles,
    dims,
    lat_ref,
    start_ref,
    cached_ref,
    shift_ref,
    scale_ref,
    gate_ref,
    sizes_ref,
    conv_ref,
    near_ref,
    wqkv_ref,
    qg_ref,
    kg_ref,
    wt_ref,
    upd_ref,
    vel_ref,
    nbuf,
    wbuf,
    kvbuf,
    qbuf,
    abuf,
    gbuf,
    cbuf,
    sbuf,
    pbuf,
    xsend,
    xrecv,
    ssend,
    srecv,
    vbuf,
    ubuf,
    w_sem,
    in_sem,
    n_sem,
    kv_send,
    kv_recv,
    g_send,
    g_recv,
    x_sem,
    s_sem,
    out_sem,
):
    lz, ly, lx = dims
    s = lax.axis_index("step")
    t = lax.axis_index("tile")
    other = 1 - s
    zc, yc, xc = t // (ly * lx), lax.rem(t // lx, ly), lax.rem(t, lx)
    col, row = lax.rem(t, GRID_COLS), t // GRID_COLS
    rows = tiles // GRID_COLS
    tok, width = lat_ref.shape[1], lat_ref.shape[2]
    chunks, cw = kvbuf.shape[1], kvbuf.shape[4]
    hd = qg_ref.shape[1]
    heads = cw // hd
    relay = lx == 2 and ly == 2 and GRID_COLS == 4
    planes = lz
    pcols = width // planes

    strides = (ly * lx, lx, 1)
    coords = (zc, yc, xc)
    barrier = pltpu.get_barrier_semaphore()
    links = []
    for d in range(3):
        covered = strides[d] == GRID_COLS or (strides[d] == 1 and not relay)
        if dims[d] > 1 and not covered:
            links.append((coords[d] < dims[d] - 1, t + strides[d]))
            links.append((coords[d] > 0, t - strides[d]))
    if not relay:
        links.append((col < GRID_COLS - 1, t + 1))
        links.append((col > 0, t - 1))
    links.append((row < rows - 1, t + GRID_COLS))
    links.append((row > 0, t - GRID_COLS))
    pl.semaphore_signal(barrier, inc=1, device_id={"step": other}, device_id_type=MESH)
    for valid, peer in links:

        @pl.when(valid)
        def _(peer=peer):
            pl.semaphore_signal(barrier, inc=1, device_id={"tile": peer}, device_id_type=MESH)

    def w_copy(i):
        return pltpu.make_async_copy(
            wqkv_ref.at[i % 3, :, pl.ds((i // 3) * cw, cw)], wbuf.at[i % 3, i // 3], w_sem.at[i]
        )

    for c in range(chunks):
        w_copy(3 * c + 1).start()
        w_copy(3 * c + 2).start()
    for c in range(chunks):
        w_copy(3 * c).start()
    hw = gbuf.shape[3]
    own_w = [
        pltpu.make_async_copy(wt_ref.at[:, pl.ds(h * hw, hw)], gbuf.at[h, t], in_sem.at[h])
        for h in range(2)
    ]
    for copy in own_w:
        copy.start()
    cached_copy = pltpu.make_async_copy(cached_ref.at[0], cbuf, in_sem.at[2])
    start_copy = pltpu.make_async_copy(start_ref, sbuf, in_sem.at[3])
    cached_copy.start()
    start_copy.start()

    pl.semaphore_wait(barrier, 1 + sum(valid.astype(jnp.int32) for valid, _ in links))

    orders = ((0, 1, 2), (0, 2, 1))
    lines = [nearest(coords[d], dims[d]) for d in range(3)]

    def g_copy(h, source, src, d, up):
        peer = t + strides[d] if up else t - strides[d]
        return pltpu.make_async_remote_copy(
            src_ref=src,
            dst_ref=gbuf.at[h, source],
            send_sem=g_send.at[h, source, 2 * d + (1 if up else 0)],
            recv_sem=g_recv.at[h, source],
            device_id={"tile": peer},
            device_id_type=MESH,
        )

    def g_each(offset, act):
        source = sum(lines[d][offset[d]] * strides[d] for d in range(3))
        for h in range(2):
            order = orders[h]
            for j in range(3):
                d = order[j]
                if any(offset[e] != 0 for e in order[j + 1 :]):
                    continue
                for up in (True, False):
                    if up:
                        valid = coords[d] < dims[d] - 1
                    else:
                        valid = coords[d] > 0
                    if offset[d] != 0:
                        if dims[d] == 2:
                            continue
                        place = lines[d][offset[d]]
                        away = coords[d] > place if up else coords[d] < place
                        valid = jnp.logical_and(valid, away)

                    @pl.when(valid)
                    def _(h=h, d=d, up=up):
                        own = offset == (0, 0, 0)
                        src = wt_ref.at[:, pl.ds(h * hw, hw)] if own else gbuf.at[h, source]
                        act(g_copy(h, source, src, d, up))

    def g_step(offset):
        if offset != (0, 0, 0):
            source = sum(lines[d][offset[d]] * strides[d] for d in range(3))
            for h in range(2):
                pltpu.make_async_remote_copy(
                    src_ref=gbuf.at[h, source],
                    dst_ref=gbuf.at[h, source],
                    send_sem=g_send.at[h, source, 0],
                    recv_sem=g_recv.at[h, source],
                    device_id={"step": other},
                    device_id_type=MESH,
                ).wait_recv()
        g_each(offset, lambda copy: copy.start())

    offsets = [
        (a, b, c)
        for a in range(dims[0])
        for b, c in sorted(
            [(b, c) for b in range(dims[1]) for c in range(dims[2])], key=lambda v: v[0] + v[1]
        )
    ]
    g_step((0, 0, 0))

    def n_copy(part):
        half = tok // 2
        where = nbuf.at[s, pl.ds(part * half, half)]
        return pltpu.make_async_remote_copy(
            src_ref=where,
            dst_ref=where,
            send_sem=n_sem.at[0, part],
            recv_sem=n_sem.at[1, part],
            device_id={"step": other},
            device_id_type=MESH,
        )

    for part in range(2):
        half = tok // 2
        own = lat_ref[0, pl.ds(part * half, half), :]
        mean = jnp.mean(own, axis=-1, keepdims=True)
        cent = own - mean
        var = jnp.mean(cent * cent, axis=-1, keepdims=True)
        normed = cent / jnp.sqrt(var + 1e-06) * (1.0 + scale_ref[...]) + shift_ref[...]
        nbuf[s, pl.ds(part * half, half), :] = normed.astype(BF16)
        n_copy(part).start()

    present = (None, col > 0, col < GRID_COLS - 1, row > 0, row < rows - 1)
    for j in range(1, 5):

        @pl.when(jnp.logical_not(present[j]))
        def _(j=j):
            @pl.loop(0, chunks)
            def _(c):
                kvbuf[j, c] = jnp.zeros(kvbuf.shape[2:], BF16)

    for part in range(2):
        n_copy(part).wait()

    def kv_copy(src_slot, slot, sem, c, peer):
        return pltpu.make_async_remote_copy(
            src_ref=kvbuf.at[src_slot, c],
            dst_ref=kvbuf.at[slot, c],
            send_sem=kv_send.at[sem, c],
            recv_sem=kv_recv.at[slot, c],
            device_id={"tile": peer},
            device_id_type=MESH,
        )

    right, left = col < GRID_COLS - 1, col > 0
    if relay:
        right, left = lax.rem(col, 2) == 0, lax.rem(col, 2) == 1
    sends = (
        (1, right, t + 1),
        (2, left, t - 1),
        (3, row < rows - 1, t + GRID_COLS),
        (4, row > 0, t - GRID_COLS),
    )

    def kv_sends(c, act):
        for slot, valid, peer in sends:

            @pl.when(valid)
            def _(slot=slot, peer=peer):
                act(kv_copy(0, slot, slot, c, peer))

    passed = ((2, 1, col == 0, t + 2), (1, 2, col == 3, t - 2))

    def kv_wait(c, slots):
        for slot in slots:

            @pl.when(present[slot])
            def _(slot=slot):
                pltpu.make_async_remote_copy(
                    src_ref=kvbuf.at[slot, c],
                    dst_ref=kvbuf.at[slot, c],
                    send_sem=kv_send.at[slot, c],
                    recv_sem=kv_recv.at[slot, c],
                    device_id={"step": other},
                    device_id_type=MESH,
                ).wait_recv()

    def kv_pass(c):
        if not relay:
            return
        for slot, onward, valid, peer in passed:

            @pl.when(lax.rem(col, 2) == (0 if slot == 2 else 1))
            def _(slot=slot):
                pltpu.make_async_remote_copy(
                    src_ref=kvbuf.at[slot, c],
                    dst_ref=kvbuf.at[slot, c],
                    send_sem=kv_send.at[slot, c],
                    recv_sem=kv_recv.at[slot, c],
                    device_id={"step": other},
                    device_id_type=MESH,
                ).wait_recv()

            @pl.when(valid)
            def _(slot=slot, onward=onward, peer=peer):
                kv_copy(slot, onward, 0, c, peer).start()

    def kv_rest(c):
        if not relay:
            kv_wait(c, (1, 2, 3, 4))
            return
        for slot, valid in ((1, col == 2), (2, col == 1)):

            @pl.when(valid)
            def _(slot=slot):
                pltpu.make_async_remote_copy(
                    src_ref=kvbuf.at[slot, c],
                    dst_ref=kvbuf.at[slot, c],
                    send_sem=kv_send.at[slot, c],
                    recv_sem=kv_recv.at[slot, c],
                    device_id={"step": other},
                    device_id_type=MESH,
                ).wait_recv()

        kv_wait(c, (3, 4))

    def project(which, c):
        block = nbuf[...].reshape(2 * tok, width)
        return jnp.dot(block, wbuf[which, c], preferred_element_type=F32)

    def rms(result, gain):
        parts = []
        for h in range(heads):
            part = result[:, h * hd : (h + 1) * hd]
            square = jnp.mean(part * part, axis=-1, keepdims=True)
            parts.append(part / jnp.sqrt(square + 1e-06) * gain)
        return jnp.concatenate(parts, axis=-1).astype(BF16)

    def w_wait(which, c):
        pltpu.make_async_copy(
            wqkv_ref.at[which, :, pl.ds(0, cw)], wbuf.at[which, c], w_sem.at[3 * c + which]
        ).wait()

    @pl.loop(0, chunks)
    def _(c):
        w_wait(1, c)
        kvbuf[0, c, 0] = rms(project(1, c), kg_ref[...])
        w_wait(2, c)
        kvbuf[0, c, 1] = project(2, c).astype(BF16)
        kv_sends(c, lambda copy: copy.start())

    for offset in offsets[1 : ly * lx]:
        g_step(offset)

    @pl.loop(0, chunks)
    def _(c):
        w_wait(0, c)
        qbuf[c] = rms(project(0, c), qg_ref[...])

    factor = 1.0 / jnp.sqrt(jnp.float32(hd))
    ones = jnp.ones((1, tok), F32)
    mask = jnp.concatenate(
        [ones] + [ones * near_ref[0, j].astype(F32) for j in range(4)], axis=1
    )
    per_half = abuf.shape[3] // cw

    def attention(c):
        @pl.loop(0, 2)
        def _(k):
            at = pl.ds(pl.multiple_of(k * tok, tok), tok)
            for h in range(heads):
                cols = pl.ds(h * hd, hd)
                q = qbuf[c, at, cols]
                keys = kvbuf[:, c, 0, at, cols].reshape(5 * tok, hd)
                values = kvbuf[:, c, 1, at, cols].reshape(5 * tok, hd)
                scores = lax.dot_general(
                    q, keys, (((1,), (1,)), ((), ())), preferred_element_type=F32
                )
                expo = jnp.exp(scores * factor) * mask
                probs = (expo / jnp.sum(expo, axis=-1, keepdims=True)).astype(BF16)
                out = jnp.dot(probs, values, preferred_element_type=F32)
                abuf[c // per_half, k, :, pl.ds((c % per_half) * cw + h * hd, hd)] = out.astype(
                    BF16
                )

    plane = ly * lx
    later = [g for a in range(1, lz) for g in offsets[a * plane : (a + 1) * plane]]
    todo = list(later)
    kv_pass(0)
    g_step(todo.pop(0))
    kv_pass(1)
    kv_pass(2)
    for offset in [todo.pop(0) for _ in range(min(2, len(todo)))]:
        g_step(offset)
    kv_pass(3) if chunks > 3 else None
    for c in range(4, chunks):
        kv_pass(c)
    for c in range(chunks):
        kv_rest(c)
        attention(c)
        if todo:
            g_step(todo.pop(0))

    for copy in own_w:
        copy.wait()
    cached_copy.wait()
    start_copy.wait()
    flag = conv_ref[s, 0] > 0

    def x_copy(k):
        return pltpu.make_async_remote_copy(
            src_ref=xsend.at[k],
            dst_ref=xrecv.at[k],
            send_sem=x_sem.at[0, k],
            recv_sem=x_sem.at[1, k],
            device_id={"step": other},
            device_id_type=MESH,
        )

    def s_copy(k):
        return pltpu.make_async_remote_copy(
            src_ref=ssend.at[k],
            dst_ref=srecv.at[k],
            send_sem=s_sem.at[0, k],
            recv_sem=s_sem.at[1, k],
            device_id={"step": other},
            device_id_type=MESH,
        )

    def at_cols(k):
        return pl.ds(pl.multiple_of(lines[0][k] * pcols, 128), pcols)

    def out_copy(k, which):
        src, dst = ((ubuf, upd_ref), (vbuf, vel_ref))[which]
        return pltpu.make_async_copy(src.at[k], dst.at[0, :, at_cols(k)], out_sem.at[which, k])

    def out_dot(k):
        which = pl.ds(lines[0][k] * plane, plane)
        total = None
        for h in range(2):
            weights = gbuf[h, which].reshape(pcols, gbuf.shape[3])
            block = abuf[h].reshape(2 * tok, gbuf.shape[3])
            term = lax.dot_general(
                block, weights, (((1,), (1,)), ((), ())), preferred_element_type=F32
            )
            total = term if total is None else total + term
        pbuf[k] = total.reshape(2, tok, pcols)
        xsend[k] = pbuf[k, other].astype(BF16)
        x_copy(k).start()

    def finish(k):
        x_copy(k).wait()
        projected = pbuf[k, s] + xrecv[k].astype(F32)
        velocity = jnp.where(flag, cbuf[:, at_cols(k)], gate_ref[:, at_cols(k)] * projected)
        vbuf[k] = velocity
        out_copy(k, 1).start()

        @pl.when(s == 0)
        def _():
            ssend[k] = (sizes_ref[0] * velocity).astype(BF16)
            s_copy(k).start()
            ubuf[k] = sbuf[:, at_cols(k)]
            out_copy(k, 0).start()

    def finish_later(k):
        @pl.when(s == 1)
        def _():
            s_copy(k).wait_recv()
            ubuf[k] = sbuf[:, at_cols(k)] + srecv[k].astype(F32)
            out_copy(k, 0).start()

    for k in range(planes):
        while len(todo) > (planes - 1 - k) * plane:
            g_step(todo.pop(0))
        out_dot(k)
        if k >= 1:
            finish(k - 1)
        if k >= 2:
            finish_later(k - 2)
    finish(planes - 1)
    if planes >= 2:
        finish_later(planes - 2)
    finish_later(planes - 1)

    for offset in offsets:
        g_each(offset, lambda copy: copy.wait_send())

    @pl.loop(0, chunks)
    def _(c):
        kv_sends(c, lambda copy: copy.wait_send())
        if relay:
            for slot, onward, valid, peer in passed:

                @pl.when(valid)
                def _(slot=slot, onward=onward, peer=peer):
                    kv_copy(slot, onward, 0, c, peer).wait_send()

    @pl.when(s == 0)
    def _():
        for k in range(planes):
            s_copy(k).wait_send()

    for k in range(planes):
        out_copy(k, 0).wait()
        out_copy(k, 1).wait()


def split(tiles):
    side = int(round((tiles // 4) ** 0.5))
    assert 4 * side * side == tiles
    return (4, side, side)


def body(tiles, *args):
    (
        latents,
        start,
        cached_velocity,
        shift,
        scale,
        gate,
        step_sizes,
        converged,
        neighbours,
        w_qkv,
        q_gain,
        k_gain,
        w_out,
    ) = args
    tok, width = latents.shape[1], latents.shape[2]
    group = w_qkv.shape[2]
    hd = q_gain.shape[0]
    shard = w_out.shape[1]
    dims = split(tiles)
    planes = dims[0]
    pcols = width // planes
    cw = 2 * hd
    chunks = group // cw
    wt = w_out.T
    any_space = pl.BlockSpec(memory_space=pl.ANY)
    vmem = pl.BlockSpec(memory_space=pltpu.VMEM)
    smem = pl.BlockSpec(memory_space=pltpu.SMEM)
    dma = pltpu.SemaphoreType.DMA
    upd, vel = pl.pallas_call(
        functools.partial(kernel, tiles, dims),
        out_shape=[jax.ShapeDtypeStruct((1, tok, width), F32)] * 2,
        in_specs=[
            vmem,
            any_space,
            any_space,
            vmem,
            vmem,
            vmem,
            smem,
            smem,
            smem,
            any_space,
            vmem,
            vmem,
            any_space,
        ],
        out_specs=[any_space, any_space],
        scratch_shapes=[
            pltpu.VMEM((2, tok, width), BF16),
            pltpu.VMEM((3, chunks, width, cw), BF16),
            pltpu.VMEM((5, chunks, 2, 2 * tok, cw), BF16),
            pltpu.VMEM((chunks, 2 * tok, cw), BF16),
            pltpu.VMEM((2, 2, tok, group // 2), BF16),
            pltpu.VMEM((2, tiles, shard, group // 2), BF16),
            pltpu.VMEM((tok, width), F32),
            pltpu.VMEM((tok, width), F32),
            pltpu.VMEM((planes, 2, tok, pcols), F32),
            pltpu.VMEM((planes, tok, pcols), BF16),
            pltpu.VMEM((planes, tok, pcols), BF16),
            pltpu.VMEM((planes, tok, pcols), BF16),
            pltpu.VMEM((planes, tok, pcols), BF16),
            pltpu.VMEM((planes, tok, pcols), F32),
            pltpu.VMEM((planes, tok, pcols), F32),
            dma((3 * chunks,)),
            dma((4,)),
            dma((2, 2)),
            dma((5, chunks)),
            dma((5, chunks)),
            dma((2, tiles, 6)),
            dma((2, tiles)),
            dma((2, planes)),
            dma((2, planes)),
            dma((2, planes)),
        ],
        compiler_params=pltpu.CompilerParams(
            collective_id=0, has_side_effects=True, vmem_limit_bytes=60 * 1024 * 1024
        ),
    )(
        latents,
        start,
        cached_velocity,
        shift,
        scale,
        gate,
        step_sizes,
        converged,
        neighbours,
        w_qkv,
        q_gain[None],
        k_gain[None],
        wt,
    )
    return (upd, vel)


def solution(mesh):
    assert mesh.shape["step"] == 2
    placed = (
        P("step", "tile", None),
        P("tile", None),
        P("step", "tile", None),
        P("step", None),
        P("step", None),
        P("step", None),
        P("step"),
        P(None, "tile"),
        P("tile", None),
        P(None, None, "step"),
        P(),
        P(),
        P("step", "tile"),
    )
    return jax.shard_map(
        functools.partial(body, mesh.shape["tile"]),
        mesh=mesh,
        in_specs=placed,
        out_specs=(P("step", "tile", None), P("step", "tile", None)),
        check_vma=False,
    )
```

time: 184 us -> 133 us (0.72)
  Pallas kernels: 0 us -> 126 us
  waiting for transfers between devices: 102 us -> 0 us
  matrix products: 19.4 us -> 0 us
  local copies, waits for them, and re-layouts: 21.4 us -> 5.26 us
  between operations: 16.8 us -> 1.29 us
  other arithmetic: 11.8 us -> 0 us
  starting transfers between devices: 10.8 us -> 0 us
    pallas_call x0 -> x1, Pallas kernels: none -> 126 us  [body(): pl.pallas_call(functools.partial(kernel, tiles, dims), out_shape=[jax.Sha...]
    all_gather x3 -> x0, waiting for transfers between devices: 46.9 us -> none  [the longest x1 24.6 us: body(): lax.all_gather(w_out, 'tile', axis=1, tiled=True)]
    ppermute x4 -> x0, waiting for transfers between devices: 46.5 us -> none  [shifted(): lax.ppermute(value, axis, [(source, source + steps) for source in range(f...]
    dot_general x4 -> x0, matrix products: 19.4 us -> none  [the longest x1 9.43 us: body(): jnp.einsum('rd,cdf->crf', project_flat, w_qkv, preferred_element_type=jnp...]
    ppermute x4 -> x0, starting transfers between devices: 10.7 us -> none  [shifted(): lax.ppermute(value, axis, [(source, source + steps) for source in range(f...]
    reduce_scatter x1 -> x0, waiting for transfers between devices: 8.22 us -> none  [body(): lax.psum_scatter(terms.astype(jnp.bfloat16), 'step', scatter_dimension=0,...]
    another operation x2 -> x0, local copies, waits for them, and re-layouts: 7.93 us -> none
    convert_element_type x5 -> x0, other arithmetic: 4.61 us -> none  [the longest x1 2.82 us: entering(): gathered = lax.all_gather(value.astype(jnp.bfloat16), axis)]
  transfers between devices with their start and end apart: 8 -> 0, of which waited for: 5 -> 0; matrix products, arithmetic and copies ran while one was open for 21% -> 0% of each run, Pallas kernels for 0% -> 0%
where the time goes in v1:
time: 133 us
  Pallas kernels  126 us (95%)
  local copies, waits for them, and re-layouts  5.26 us (4%)
    pallas_call x1, Pallas kernels, body(): pl.pallas_call(functools.partial(kernel, tiles, dims), out_shape=[jax.Sha...  126 us
    unnamed x5, local copies, waits for them, and re-layouts  5.26 us

profile of v1, /device:TPU:3, one launch (start us, length us, event | category | flops | bytes accessed | tf_op | source)
XLA Modules:
  0.0 132.5 jit_solution(10280091426270817039)
XLA Ops:
  1.3 1.3 copy.15.conv_ref
  2.6 126.0 %shard_map.140 = (f32[1,128,3072]{2,1,0:T(8,128)}, f32[1,128,3072]{2,1,0:T(8,128)}) custom-call(f32[1,128,3072]{2,1,0:T(8,128)} %lat_ref.1, f32[128,3072]{1,0:T(8,128)} %start_ref.1, f32[1,128,3072]{2,1,0:T(8,128)} %cached_ref.1, f32[1,3072]{1,0:T(1,128)} %shift_ref.1, f32[1,3072]{1,0:T(1,128)} %scale_ref.1, f32[1,3072]{1,0:T(1,128)} %gate_ref.1, ...), custom_call_target="tpu_custom_call" | custom-call | tf_op jit(solution)/shard_map/pallas_call | solution.py:532
  128.6 0.0 copy-start
  128.6 2.8 %copy.19 = f32[1,128,3072]{2,1,0:T(8,128)} copy(f32[1,128,3072]{2,1,0:T(8,128)} %get-tuple-element.4) | data formatting | bytes 3145728
  131.4 0.0 copy-done
  131.4 1.1 copy.20
Async XLA Ops:
  128.6 2.8 %copy-start = (f32[1,128,3072]{2,1,0:T(8,128)S(1)}, f32[1,128,3072]{2,1,0:T(8,128)}, u32[]{:S(2)}) copy-start(f32[1,128,3072]{2,1,0:T(8,128)} %get-tuple-element.5) | copy-start | bytes 4718596

commit v2 on v1

--- a/solution.py
+++ b/solution.py
@@ -52,6 +52,7 @@
     kvbuf,
     qbuf,
     abuf,
+    apeer,
     gbuf,
     cbuf,
     sbuf,
@@ -60,6 +61,8 @@
     xrecv,
     ssend,
     srecv,
+    ysend,
+    yrecv,
     vbuf,
     ubuf,
     w_sem,
@@ -71,6 +74,8 @@
     g_recv,
     x_sem,
     s_sem,
+    a_sem,
+    y_sem,
     out_sem,
 ):
     lz, ly, lx = dims
@@ -85,8 +90,11 @@
     hd = qg_ref.shape[1]
     heads = cw // hd
     relay = lx == 2 and ly == 2 and GRID_COLS == 4
+    pair = ly == 2
     planes = lz
-    pcols = width // planes
+    groups = 2 if pair else 1
+    pcols = width // planes // groups
+    plane = lx if pair else ly * lx
 
     strides = (ly * lx, lx, 1)
     coords = (zc, yc, xc)
@@ -120,8 +128,12 @@
     for c in range(chunks):
         w_copy(3 * c).start()
     hw = gbuf.shape[3]
+
+    def spot(tile):
+        return (tile // (ly * lx)) * lx + lax.rem(tile, lx) if pair else tile
+
     own_w = [
-        pltpu.make_async_copy(wt_ref.at[:, pl.ds(h * hw, hw)], gbuf.at[h, t], in_sem.at[h])
+        pltpu.make_async_copy(wt_ref.at[:, pl.ds(h * hw, hw)], gbuf.at[h, spot(t)], in_sem.at[h])
         for h in range(2)
     ]
     for copy in own_w:
@@ -133,16 +145,16 @@
 
     pl.semaphore_wait(barrier, 1 + sum(valid.astype(jnp.int32) for valid, _ in links))
 
-    orders = ((0, 1, 2), (0, 2, 1))
+    orders = ((0, 2), (0, 2)) if pair else ((0, 1, 2), (0, 2, 1))
     lines = [nearest(coords[d], dims[d]) for d in range(3)]
 
     def g_copy(h, source, src, d, up):
         peer = t + strides[d] if up else t - strides[d]
         return pltpu.make_async_remote_copy(
             src_ref=src,
-            dst_ref=gbuf.at[h, source],
-            send_sem=g_send.at[h, source, 2 * d + (1 if up else 0)],
-            recv_sem=g_recv.at[h, source],
+            dst_ref=gbuf.at[h, spot(source)],
+            send_sem=g_send.at[h, spot(source), 2 * d + (1 if up else 0)],
+            recv_sem=g_recv.at[h, spot(source)],
             device_id={"tile": peer},
             device_id_type=MESH,
         )
@@ -151,7 +163,7 @@
         source = sum(lines[d][offset[d]] * strides[d] for d in range(3))
         for h in range(2):
             order = orders[h]
-            for j in range(3):
+            for j in range(len(order)):
                 d = order[j]
                 if any(offset[e] != 0 for e in order[j + 1 :]):
                     continue
@@ -170,7 +182,7 @@
                     @pl.when(valid)
                     def _(h=h, d=d, up=up):
                         own = offset == (0, 0, 0)
-                        src = wt_ref.at[:, pl.ds(h * hw, hw)] if own else gbuf.at[h, source]
+                        src = wt_ref.at[:, pl.ds(h * hw, hw)] if own else gbuf.at[h, spot(source)]
                         act(g_copy(h, source, src, d, up))
 
     def g_step(offset):
@@ -178,10 +190,10 @@
             source = sum(lines[d][offset[d]] * strides[d] for d in range(3))
             for h in range(2):
                 pltpu.make_async_remote_copy(
-                    src_ref=gbuf.at[h, source],
-                    dst_ref=gbuf.at[h, source],
-                    send_sem=g_send.at[h, source, 0],
-                    recv_sem=g_recv.at[h, source],
+                    src_ref=gbuf.at[h, spot(source)],
+                    dst_ref=gbuf.at[h, spot(source)],
+                    send_sem=g_send.at[h, spot(source), 0],
+                    recv_sem=g_recv.at[h, spot(source)],
                     device_id={"step": other},
                     device_id_type=MESH,
                 ).wait_recv()
@@ -191,7 +203,7 @@
         (a, b, c)
         for a in range(dims[0])
         for b, c in sorted(
-            [(b, c) for b in range(dims[1]) for c in range(dims[2])], key=lambda v: v[0] + v[1]
+            [(b, c) for b in range(1 if pair else dims[1]) for c in range(dims[2])], key=lambda v: v[0] + v[1]
         )
     ]
     g_step((0, 0, 0))
@@ -329,21 +341,43 @@
             wqkv_ref.at[which, :, pl.ds(0, cw)], wbuf.at[which, c], w_sem.at[3 * c + which]
         ).wait()
 
-    @pl.loop(0, chunks)
-    def _(c):
-        w_wait(1, c)
-        kvbuf[0, c, 0] = rms(project(1, c), kg_ref[...])
-        w_wait(2, c)
-        kvbuf[0, c, 1] = project(2, c).astype(BF16)
-        kv_sends(c, lambda copy: copy.start())
-
-    for offset in offsets[1 : ly * lx]:
-        g_step(offset)
-
-    @pl.loop(0, chunks)
-    def _(c):
-        w_wait(0, c)
-        qbuf[c] = rms(project(0, c), qg_ref[...])
+    def keys_values(first, last):
+        @pl.loop(first, last)
+        def _(c):
+            w_wait(1, c)
+            kvbuf[0, c, 0] = rms(project(1, c), kg_ref[...])
+            w_wait(2, c)
+            kvbuf[0, c, 1] = project(2, c).astype(BF16)
+            kv_sends(c, lambda copy: copy.start())
+
+    def query(first, last):
+        @pl.loop(first, last)
+        def _(c):
+            w_wait(0, c)
+            qbuf[c] = rms(project(0, c), qg_ref[...])
+
+    if pair:
+        forward = [(a, 0, 0) for a in range(1, lz)]
+        todo = []
+        keys_values(0, chunks // 2)
+        g_step(forward[0])
+        keys_values(chunks // 2, chunks)
+        query(0, chunks // 2)
+        g_step(forward[1])
+        kv_pass(0)
+        query(chunks // 2, chunks)
+        kv_pass(1)
+        g_step(forward[2])
+        for c in range(2, chunks):
+            kv_pass(c)
+    else:
+        keys_values(0, chunks)
+        for offset in offsets[1:plane]:
+            g_step(offset)
+        query(0, chunks)
+        todo = [g for a in range(1, lz) for g in offsets[a * plane : (a + 1) * plane]]
+        for c in range(chunks):
+            kv_pass(c)
 
     factor = 1.0 / jnp.sqrt(jnp.float32(hd))
     ones = jnp.ones((1, tok), F32)
@@ -371,29 +405,29 @@
                     BF16
                 )
 
-    plane = ly * lx
-    later = [g for a in range(1, lz) for g in offsets[a * plane : (a + 1) * plane]]
-    todo = list(later)
-    kv_pass(0)
-    g_step(todo.pop(0))
-    kv_pass(1)
-    kv_pass(2)
-    for offset in [todo.pop(0) for _ in range(min(2, len(todo)))]:
-        g_step(offset)
-    kv_pass(3) if chunks > 3 else None
-    for c in range(4, chunks):
-        kv_pass(c)
+    def a_copy(h):
+        return pltpu.make_async_remote_copy(
+            src_ref=abuf.at[h],
+            dst_ref=apeer.at[h],
+            send_sem=a_sem.at[0, h],
+            recv_sem=a_sem.at[1, h],
+            device_id={"tile": t + (1 - 2 * yc) * lx},
+            device_id_type=MESH,
+        )
+
     for c in range(chunks):
         kv_rest(c)
         attention(c)
-        if todo:
+        if pair and (c + 1) % per_half == 0:
+            a_copy(c // per_half).start()
+        if not pair and todo:
             g_step(todo.pop(0))
 
     for copy in own_w:
         copy.wait()
     cached_copy.wait()
     start_copy.wait()
-    flag = conv_ref[s, 0] > 0
+    flag = conv_ref[0, s] > 0
 
     def x_copy(k):
         return pltpu.make_async_remote_copy(
@@ -415,60 +449,93 @@
             device_id_type=MESH,
         )
 
-    def at_cols(k):
-        return pl.ds(pl.multiple_of(lines[0][k] * pcols, 128), pcols)
-
-    def out_copy(k, which):
+    def y_copy(k):
+        return pltpu.make_async_remote_copy(
+            src_ref=ysend.at[k],
+            dst_ref=yrecv.at[k],
+            send_sem=y_sem.at[0, k],
+            recv_sem=y_sem.at[1, k],
+            device_id={"tile": t + (1 - 2 * yc) * lx},
+            device_id_type=MESH,
+        )
+
+    def at_cols(b):
+        block = lines[0][b // groups]
+        if pair:
+            block = 2 * block + (yc if b % 2 == 0 else 1 - yc)
+        return pl.ds(pl.multiple_of(block * pcols, 128), pcols)
+
+    def out_copy(b, which):
         src, dst = ((ubuf, upd_ref), (vbuf, vel_ref))[which]
-        return pltpu.make_async_copy(src.at[k], dst.at[0, :, at_cols(k)], out_sem.at[which, k])
+        return pltpu.make_async_copy(src.at[b], dst.at[0, :, at_cols(b)], out_sem.at[which, b])
 
     def out_dot(k):
         which = pl.ds(lines[0][k] * plane, plane)
-        total = None
-        for h in range(2):
-            weights = gbuf[h, which].reshape(pcols, gbuf.shape[3])
-            block = abuf[h].reshape(2 * tok, gbuf.shape[3])
-            term = lax.dot_general(
-                block, weights, (((1,), (1,)), ((), ())), preferred_element_type=F32
-            )
-            total = term if total is None else total + term
-        pbuf[k] = total.reshape(2, tok, pcols)
-        xsend[k] = pbuf[k, other].astype(BF16)
+        for who in range(groups):
+            total = None
+            for h in range(2):
+                weights = gbuf[h, which].reshape(pcols, hw)
+                block = (abuf, apeer)[who][h].reshape(2 * tok, hw)
+                term = lax.dot_general(
+                    block, weights, (((1,), (1,)), ((), ())), preferred_element_type=F32
+                )
+                total = term if total is None else total + term
+            pbuf[k, who] = total.reshape(2, tok, pcols)
+            xsend[k, who] = pbuf[k, who, other].astype(BF16)
         x_copy(k).start()
 
-    def finish(k):
-        x_copy(k).wait()
-        projected = pbuf[k, s] + xrecv[k].astype(F32)
-        velocity = jnp.where(flag, cbuf[:, at_cols(k)], gate_ref[:, at_cols(k)] * projected)
-        vbuf[k] = velocity
-        out_copy(k, 1).start()
+    def finish(b, projected):
+        velocity = jnp.where(flag, cbuf[:, at_cols(b)], gate_ref[:, at_cols(b)] * projected)
+        vbuf[b] = velocity
+        out_copy(b, 1).start()
 
         @pl.when(s == 0)
         def _():
-            ssend[k] = (sizes_ref[0] * velocity).astype(BF16)
-            s_copy(k).start()
-            ubuf[k] = sbuf[:, at_cols(k)]
-            out_copy(k, 0).start()
-
-    def finish_later(k):
+            ssend[b] = (sizes_ref[0] * velocity).astype(BF16)
+            s_copy(b).start()
+            ubuf[b] = sbuf[:, at_cols(b)]
+            out_copy(b, 0).start()
+
+    def finish_own(k):
+        x_copy(k).wait()
+        if pair:
+            ysend[k] = (pbuf[k, 1, s] + xrecv[k, 1].astype(F32)).astype(BF16)
+            y_copy(k).start()
+        finish(groups * k, pbuf[k, 0, s] + xrecv[k, 0].astype(F32))
+
+    def finish_peer(k):
+        if pair:
+            y_copy(k).wait()
+            finish(2 * k + 1, yrecv[k].astype(F32))
+
+    def finish_later(b):
         @pl.when(s == 1)
         def _():
-            s_copy(k).wait_recv()
-            ubuf[k] = sbuf[:, at_cols(k)] + srecv[k].astype(F32)
-            out_copy(k, 0).start()
-
+            s_copy(b).wait_recv()
+            ubuf[b] = sbuf[:, at_cols(b)] + srecv[b].astype(F32)
+            out_copy(b, 0).start()
+
+    if pair:
+        for h in range(2):
+            a_copy(h).wait()
     for k in range(planes):
-        while len(todo) > (planes - 1 - k) * plane:
-            g_step(todo.pop(0))
+        if pair:
+            g_step((k, 0, 1))
+        else:
+            while len(todo) > (planes - 1 - k) * plane:
+                g_step(todo.pop(0))
         out_dot(k)
         if k >= 1:
-            finish(k - 1)
+            finish_own(k - 1)
         if k >= 2:
-            finish_later(k - 2)
-    finish(planes - 1)
-    if planes >= 2:
-        finish_later(planes - 2)
-    finish_later(planes - 1)
+            finish_peer(k - 2)
+            for b in range(groups * (k - 2), groups * (k - 1)):
+                finish_later(b)
+    finish_own(planes - 1)
+    finish_peer(planes - 2)
+    finish_peer(planes - 1)
+    for b in range(groups * (planes - 2), groups * planes):
+        finish_later(b)
 
     for offset in offsets:
         g_each(offset, lambda copy: copy.wait_send())
@@ -485,12 +552,12 @@
 
     @pl.when(s == 0)
     def _():
-        for k in range(planes):
-            s_copy(k).wait_send()
-
-    for k in range(planes):
-        out_copy(k, 0).wait()
-        out_copy(k, 1).wait()
+        for b in range(groups * planes):
+            s_copy(b).wait_send()
+
+    for b in range(groups * planes):
+        out_copy(b, 0).wait()
+        out_copy(b, 1).wait()
 
 
 def split(tiles):
@@ -521,7 +588,9 @@
     shard = w_out.shape[1]
     dims = split(tiles)
     planes = dims[0]
-    pcols = width // planes
+    groups = 2 if dims[1] == 2 else 1
+    blocks = groups * planes
+    pcols = width // blocks
     cw = 2 * hd
     chunks = group // cw
     wt = w_out.T
@@ -554,26 +623,31 @@
             pltpu.VMEM((5, chunks, 2, 2 * tok, cw), BF16),
             pltpu.VMEM((chunks, 2 * tok, cw), BF16),
             pltpu.VMEM((2, 2, tok, group // 2), BF16),
-            pltpu.VMEM((2, tiles, shard, group // 2), BF16),
+            pltpu.VMEM((2, 2, tok, group // 2), BF16),
+            pltpu.VMEM((2, tiles // groups, shard, group // 2), BF16),
             pltpu.VMEM((tok, width), F32),
             pltpu.VMEM((tok, width), F32),
-            pltpu.VMEM((planes, 2, tok, pcols), F32),
+            pltpu.VMEM((planes, groups, 2, tok, pcols), F32),
+            pltpu.VMEM((planes, groups, tok, pcols), BF16),
+            pltpu.VMEM((planes, groups, tok, pcols), BF16),
+            pltpu.VMEM((blocks, tok, pcols), BF16),
+            pltpu.VMEM((blocks, tok, pcols), BF16),
             pltpu.VMEM((planes, tok, pcols), BF16),
             pltpu.VMEM((planes, tok, pcols), BF16),
-            pltpu.VMEM((planes, tok, pcols), BF16),
-            pltpu.VMEM((planes, tok, pcols), BF16),
-            pltpu.VMEM((planes, tok, pcols), F32),
-            pltpu.VMEM((planes, tok, pcols), F32),
+            pltpu.VMEM((blocks, tok, pcols), F32),
+            pltpu.VMEM((blocks, tok, pcols), F32),
             dma((3 * chunks,)),
             dma((4,)),
             dma((2, 2)),
             dma((5, chunks)),
             dma((5, chunks)),
-            dma((2, tiles, 6)),
-            dma((2, tiles)),
+            dma((2, tiles // groups, 6)),
+            dma((2, tiles // groups)),
             dma((2, planes)),
+            dma((2, blocks)),
+            dma((2, 2)),
             dma((2, planes)),
-            dma((2, planes)),
+            dma((2, blocks)),
         ],
         compiler_params=pltpu.CompilerParams(
             collective_id=0, has_side_effects=True, vmem_limit_bytes=60 * 1024 * 1024
@@ -586,7 +660,7 @@
         scale,
         gate,
         step_sizes,
-        converged,
+        converged.T,
         neighbours,
         w_qkv,
         q_gain[None],

time: 133 us -> 104 us (0.78)
  Pallas kernels: 126 us -> 98.3 us
    pallas_call x1, Pallas kernels: 126 us -> 98.3 us  [body(): pl.pallas_call(functools.partial(kernel, tiles, dims), out_shape=[jax.Sha...]
    unnamed x5 -> x4, local copies, waits for them, and re-layouts: 5.26 us -> 3.97 us
where the time goes in v2:
time: 104 us
  Pallas kernels  98.3 us (95%)
  local copies, waits for them, and re-layouts  3.97 us (4%)
  between operations  1.3 us (1%)
    pallas_call x1, Pallas kernels, body(): pl.pallas_call(functools.partial(kernel, tiles, dims), out_shape=[jax.Sha...  98.3 us
    unnamed x4, local copies, waits for them, and re-layouts  3.97 us

profile of v2, /device:TPU:3, one launch (start us, length us, event | category | flops | bytes accessed | tf_op | source)
XLA Modules:
  0.0 103.5 jit_solution(9001570798986130968)
XLA Ops:
  1.3 98.3 %shard_map.140 = (f32[1,128,3072]{2,1,0:T(8,128)}, f32[1,128,3072]{2,1,0:T(8,128)}) custom-call(f32[1,128,3072]{2,1,0:T(8,128)} %lat_ref.1, f32[128,3072]{1,0:T(8,128)} %start_ref.1, f32[1,128,3072]{2,1,0:T(8,128)} %cached_ref.1, f32[1,3072]{1,0:T(1,128)} %shift_ref.1, f32[1,3072]{1,0:T(1,128)} %scale_ref.1, f32[1,3072]{1,0:T(1,128)} %gate_ref.1, ...), custom_call_target="tpu_custom_call" | custom-call | tf_op jit(solution)/shard_map/pallas_call | solution.py:601
  99.5 0.0 copy-start
  99.6 2.8 %copy.18 = f32[1,128,3072]{2,1,0:T(8,128)} copy(f32[1,128,3072]{2,1,0:T(8,128)} %get-tuple-element.4) | data formatting | bytes 3145728
  102.4 0.0 copy-done
  102.4 1.1 %copy.19 = f32[1,128,3072]{2,1,0:T(8,128)} copy(f32[1,128,3072]{2,1,0:T(8,128)S(1)} %copy-done) | data formatting | bytes 3145728
Async XLA Ops:
  99.5 2.8 %copy-start = (f32[1,128,3072]{2,1,0:T(8,128)S(1)}, f32[1,128,3072]{2,1,0:T(8,128)}, u32[]{:S(2)}) copy-start(f32[1,128,3072]{2,1,0:T(8,128)} %get-tuple-element.5) | copy-start | bytes 4718596

commit v3 on v2

--- a/solution.py
+++ b/solution.py
@@ -226,7 +226,7 @@
         mean = jnp.mean(own, axis=-1, keepdims=True)
         cent = own - mean
         var = jnp.mean(cent * cent, axis=-1, keepdims=True)
-        normed = cent / jnp.sqrt(var + 1e-06) * (1.0 + scale_ref[...]) + shift_ref[...]
+        normed = cent * (1.0 / jnp.sqrt(var + 1e-06)) * (1.0 + scale_ref[...]) + shift_ref[...]
         nbuf[s, pl.ds(part * half, half), :] = normed.astype(BF16)
         n_copy(part).start()
 
@@ -333,7 +333,7 @@
         for h in range(heads):
             part = result[:, h * hd : (h + 1) * hd]
             square = jnp.mean(part * part, axis=-1, keepdims=True)
-            parts.append(part / jnp.sqrt(square + 1e-06) * gain)
+            parts.append(part * (1.0 / jnp.sqrt(square + 1e-06)) * gain)
         return jnp.concatenate(parts, axis=-1).astype(BF16)
 
     def w_wait(which, c):
@@ -359,17 +359,16 @@
     if pair:
         forward = [(a, 0, 0) for a in range(1, lz)]
         todo = []
-        keys_values(0, chunks // 2)
+        keys_values(0, chunks)
+        query(0, chunks // 2)
         g_step(forward[0])
-        keys_values(chunks // 2, chunks)
-        query(0, chunks // 2)
-        g_step(forward[1])
         kv_pass(0)
         query(chunks // 2, chunks)
         kv_pass(1)
-        g_step(forward[2])
+        g_step(forward[1])
         for c in range(2, chunks):
             kv_pass(c)
+        g_step(forward[2])
     else:
         keys_values(0, chunks)
         for offset in offsets[1:plane]:
@@ -387,9 +386,8 @@
     per_half = abuf.shape[3] // cw
 
     def attention(c):
-        @pl.loop(0, 2)
-        def _(k):
-            at = pl.ds(pl.multiple_of(k * tok, tok), tok)
+        for k in range(2):
+            at = pl.ds(k * tok, tok)
             for h in range(heads):
                 cols = pl.ds(h * hd, hd)
                 q = qbuf[c, at, cols]
@@ -399,7 +397,7 @@
                     q, keys, (((1,), (1,)), ((), ())), preferred_element_type=F32
                 )
                 expo = jnp.exp(scores * factor) * mask
-                probs = (expo / jnp.sum(expo, axis=-1, keepdims=True)).astype(BF16)
+                probs = (expo * (1.0 / jnp.sum(expo, axis=-1, keepdims=True))).astype(BF16)
                 out = jnp.dot(probs, values, preferred_element_type=F32)
                 abuf[c // per_half, k, :, pl.ds((c % per_half) * cw + h * hd, hd)] = out.astype(
                     BF16

time: 104 us -> 94 us (0.904)
  Pallas kernels: 98.3 us -> 87.8 us
    pallas_call x1, Pallas kernels: 98.3 us -> 87.8 us  [body(): pl.pallas_call(functools.partial(kernel, tiles, dims), out_shape=[jax.Sha...]
where the time goes in v3:
time: 94 us; the launch traced here: 93.1 us
  Pallas kernels  87.8 us (93%)
  local copies, waits for them, and re-layouts  3.97 us (4%)
  between operations  1.3 us (1%)
    pallas_call x1, Pallas kernels, body(): pl.pallas_call(functools.partial(kernel, tiles, dims), out_shape=[jax.Sha...  87.8 us
    unnamed x4, local copies, waits for them, and re-layouts  3.97 us

profile of v3, /device:TPU:3, one launch (start us, length us, event | category | flops | bytes accessed | tf_op | source)
XLA Modules:
  0.0 93.1 jit_solution(10775225954010344316)
XLA Ops:
  1.3 87.8 %shard_map.140 = (f32[1,128,3072]{2,1,0:T(8,128)}, f32[1,128,3072]{2,1,0:T(8,128)}) custom-call(f32[1,128,3072]{2,1,0:T(8,128)} %lat_ref.1, f32[128,3072]{1,0:T(8,128)} %start_ref.1, f32[1,128,3072]{2,1,0:T(8,128)} %cached_ref.1, f32[1,3072]{1,0:T(1,128)} %shift_ref.1, f32[1,3072]{1,0:T(1,128)} %scale_ref.1, f32[1,3072]{1,0:T(1,128)} %gate_ref.1, ...), custom_call_target="tpu_custom_call" | custom-call | tf_op jit(solution)/shard_map/pallas_call | solution.py:599
  89.1 0.0 copy-start
  89.1 2.8 %copy.18 = f32[1,128,3072]{2,1,0:T(8,128)} copy(f32[1,128,3072]{2,1,0:T(8,128)} %get-tuple-element.4) | data formatting | bytes 3145728
  91.9 0.0 copy-done
  91.9 1.1 %copy.19 = f32[1,128,3072]{2,1,0:T(8,128)} copy(f32[1,128,3072]{2,1,0:T(8,128)S(1)} %copy-done) | data formatting | bytes 3145728
Async XLA Ops:
  89.1 2.8 %copy-start = (f32[1,128,3072]{2,1,0:T(8,128)S(1)}, f32[1,128,3072]{2,1,0:T(8,128)}, u32[]{:S(2)}) copy-start(f32[1,128,3072]{2,1,0:T(8,128)} %get-tuple-element.5) | copy-start | bytes 4718596

commit v4 on v3

--- a/solution.py
+++ b/solution.py
@@ -383,7 +383,6 @@
     mask = jnp.concatenate(
         [ones] + [ones * near_ref[0, j].astype(F32) for j in range(4)], axis=1
     )
-    per_half = abuf.shape[3] // cw
 
     def attention(c):
         for k in range(2):
@@ -399,9 +398,7 @@
                 expo = jnp.exp(scores * factor) * mask
                 probs = (expo * (1.0 / jnp.sum(expo, axis=-1, keepdims=True))).astype(BF16)
                 out = jnp.dot(probs, values, preferred_element_type=F32)
-                abuf[c // per_half, k, :, pl.ds((c % per_half) * cw + h * hd, hd)] = out.astype(
-                    BF16
-                )
+                abuf[c, k, :, pl.ds(h * hd, hd)] = out.astype(BF16)
 
     def a_copy(h):
         return pltpu.make_async_remote_copy(
@@ -416,8 +413,8 @@
     for c in range(chunks):
         kv_rest(c)
         attention(c)
-        if pair and (c + 1) % per_half == 0:
-            a_copy(c // per_half).start()
+        if pair:
+            a_copy(c).start()
         if not pair and todo:
             g_step(todo.pop(0))
 
@@ -427,12 +424,12 @@
     start_copy.wait()
     flag = conv_ref[0, s] > 0
 
-    def x_copy(k):
+    def x_copy(b):
         return pltpu.make_async_remote_copy(
-            src_ref=xsend.at[k],
-            dst_ref=xrecv.at[k],
-            send_sem=x_sem.at[0, k],
-            recv_sem=x_sem.at[1, k],
+            src_ref=xsend.at[b // groups, b % groups],
+            dst_ref=xrecv.at[b // groups, b % groups],
+            send_sem=x_sem.at[0, b],
+            recv_sem=x_sem.at[1, b],
             device_id={"step": other},
             device_id_type=MESH,
         )
@@ -467,20 +464,25 @@
         src, dst = ((ubuf, upd_ref), (vbuf, vel_ref))[which]
         return pltpu.make_async_copy(src.at[b], dst.at[0, :, at_cols(b)], out_sem.at[which, b])
 
-    def out_dot(k):
+    def out_dot(b):
+        k, who = b // groups, b % groups
         which = pl.ds(lines[0][k] * plane, plane)
-        for who in range(groups):
-            total = None
-            for h in range(2):
-                weights = gbuf[h, which].reshape(pcols, hw)
-                block = (abuf, apeer)[who][h].reshape(2 * tok, hw)
+        total = None
+        per_half = hw // cw
+        for h in range(2):
+            weights = gbuf[h, which].reshape(pcols, hw)
+            for i in range(per_half):
+                block = (abuf, apeer)[who][h * per_half + i].reshape(2 * tok, cw)
                 term = lax.dot_general(
-                    block, weights, (((1,), (1,)), ((), ())), preferred_element_type=F32
+                    block,
+                    weights[:, i * cw : (i + 1) * cw],
+                    (((1,), (1,)), ((), ())),
+                    preferred_element_type=F32,
                 )
                 total = term if total is None else total + term
-            pbuf[k, who] = total.reshape(2, tok, pcols)
-            xsend[k, who] = pbuf[k, who, other].astype(BF16)
-        x_copy(k).start()
+        pbuf[k, who] = total.reshape(2, tok, pcols)
+        xsend[k, who] = pbuf[k, who, other].astype(BF16)
+        x_copy(b).start()
 
     def finish(b, projected):
         velocity = jnp.where(flag, cbuf[:, at_cols(b)], gate_ref[:, at_cols(b)] * projected)
@@ -494,17 +496,20 @@
             ubuf[b] = sbuf[:, at_cols(b)]
             out_copy(b, 0).start()
 
-    def finish_own(k):
-        x_copy(k).wait()
-        if pair:
-            ysend[k] = (pbuf[k, 1, s] + xrecv[k, 1].astype(F32)).astype(BF16)
+    def reduce(b):
+        k, who = b // groups, b % groups
+        x_copy(b).wait()
+        projected = pbuf[k, who, s] + xrecv[k, who].astype(F32)
+        if who == 1:
+            ysend[k] = projected.astype(BF16)
             y_copy(k).start()
-        finish(groups * k, pbuf[k, 0, s] + xrecv[k, 0].astype(F32))
-
-    def finish_peer(k):
-        if pair:
-            y_copy(k).wait()
-            finish(2 * k + 1, yrecv[k].astype(F32))
+        else:
+            finish(b, projected)
+
+    def finish_peer(b):
+        if b % groups == 1:
+            y_copy(b // groups).wait()
+            finish(b, yrecv[b // groups].astype(F32))
 
     def finish_later(b):
         @pl.when(s == 1)
@@ -514,26 +519,30 @@
             out_copy(b, 0).start()
 
     if pair:
-        for h in range(2):
-            a_copy(h).wait()
-    for k in range(planes):
-        if pair:
-            g_step((k, 0, 1))
-        else:
-            while len(todo) > (planes - 1 - k) * plane:
+        items = [0, 1]
+        for k in range(1, planes):
+            items += [2 * k + 1, 2 * k]
+    else:
+        items = list(range(planes))
+    ready = set()
+    steps = (reduce, finish_peer, finish_later)
+    lags = (1, 3, 5)
+    for i in range(len(items) + lags[-1]):
+        if i < len(items):
+            b = items[i]
+            k = b // groups
+            if pair and k not in ready:
+                g_step((k, 0, 1))
+                ready.add(k)
+            while not pair and len(todo) > (planes - 1 - k) * plane:
                 g_step(todo.pop(0))
-        out_dot(k)
-        if k >= 1:
-            finish_own(k - 1)
-        if k >= 2:
-            finish_peer(k - 2)
-            for b in range(groups * (k - 2), groups * (k - 1)):
-                finish_later(b)
-    finish_own(planes - 1)
-    finish_peer(planes - 2)
-    finish_peer(planes - 1)
-    for b in range(groups * (planes - 2), groups * planes):
-        finish_later(b)
+            if pair and i == 1:
+                for c in range(chunks):
+                    a_copy(c).wait()
+            out_dot(b)
+        for step, lag in zip(steps, lags):
+            if 0 <= i - lag < len(items):
+                step(items[i - lag])
 
     for offset in offsets:
         g_each(offset, lambda copy: copy.wait_send())
@@ -620,8 +629,8 @@
             pltpu.VMEM((3, chunks, width, cw), BF16),
             pltpu.VMEM((5, chunks, 2, 2 * tok, cw), BF16),
             pltpu.VMEM((chunks, 2 * tok, cw), BF16),
-            pltpu.VMEM((2, 2, tok, group // 2), BF16),
-            pltpu.VMEM((2, 2, tok, group // 2), BF16),
+            pltpu.VMEM((chunks, 2, tok, cw), BF16),
+            pltpu.VMEM((chunks, 2, tok, cw), BF16),
             pltpu.VMEM((2, tiles // groups, shard, group // 2), BF16),
             pltpu.VMEM((tok, width), F32),
             pltpu.VMEM((tok, width), F32),
@@ -641,9 +650,9 @@
             dma((5, chunks)),
             dma((2, tiles // groups, 6)),
             dma((2, tiles // groups)),
-            dma((2, planes)),
             dma((2, blocks)),
-            dma((2, 2)),
+            dma((2, blocks)),
+            dma((2, chunks)),
             dma((2, planes)),
             dma((2, blocks)),
         ],

time: 94 us -> 92.5 us (0.984)
  no operation moved by 1% of the time
where the time goes in v4:
time: 92.5 us; the launch traced here: 92.3 us
  Pallas kernels  87.1 us (94%)
  local copies, waits for them, and re-layouts  3.97 us (4%)
  between operations  1.3 us (1%)
    pallas_call x1, Pallas kernels, body(): pl.pallas_call(functools.partial(kernel, tiles, dims), out_shape=[jax.Sha...  87.1 us
    unnamed x4, local copies, waits for them, and re-layouts  3.97 us

profile of v4, /device:TPU:3, one launch (start us, length us, event | category | flops | bytes accessed | tf_op | source)
XLA Modules:
  0.0 92.3 jit_solution(1699875223733284730)
XLA Ops:
  1.3 87.1 %shard_map.140 = (f32[1,128,3072]{2,1,0:T(8,128)}, f32[1,128,3072]{2,1,0:T(8,128)}) custom-call(f32[1,128,3072]{2,1,0:T(8,128)} %lat_ref.1, f32[128,3072]{1,0:T(8,128)} %start_ref.1, f32[1,128,3072]{2,1,0:T(8,128)} %cached_ref.1, f32[1,3072]{1,0:T(1,128)} %shift_ref.1, f32[1,3072]{1,0:T(1,128)} %scale_ref.1, f32[1,3072]{1,0:T(1,128)} %gate_ref.1, ...), custom_call_target="tpu_custom_call" | custom-call | tf_op jit(solution)/shard_map/pallas_call | solution.py:608
  88.3 0.0 copy-start
  88.4 2.8 %copy.18 = f32[1,128,3072]{2,1,0:T(8,128)} copy(f32[1,128,3072]{2,1,0:T(8,128)} %get-tuple-element.4) | data formatting | bytes 3145728
  91.2 0.0 copy-done
  91.2 1.1 %copy.19 = f32[1,128,3072]{2,1,0:T(8,128)} copy(f32[1,128,3072]{2,1,0:T(8,128)S(1)} %copy-done) | data formatting | bytes 3145728
Async XLA Ops:
  88.3 2.8 %copy-start = (f32[1,128,3072]{2,1,0:T(8,128)S(1)}, f32[1,128,3072]{2,1,0:T(8,128)}, u32[]{:S(2)}) copy-start(f32[1,128,3072]{2,1,0:T(8,128)} %get-tuple-element.5) | copy-start | bytes 4718596
